TPU v7x, 256 devices: a whole 4x4x8 slice. The times are simulated.
256 devices in a mesh: tile: 16 (over z, core), tm: 16 (over x, y).
Axes of the slice: x: 4, y: 4, z: 8, core: 2. Of those that a mesh axis runs over, the one named last changes fastest.
Arguments:
- src_snap: bfloat16 [256, 32, 128, 256], P('tile', 'tm'), may hold values from -6 to 6
- rcv_snap: bfloat16 [256, 32, 128, 256], P('tile', 'tm'), may hold values from -6 to 6
- q_rate: float32 [256], replicated, may hold values from 0.05 to 1.5
- nbr_device: int32 [256, 2], replicated, may hold values from 0 to 15, all different within a row; in each aligned block of 16 rows (0 to 15, 16 to 31, ...) at most 3 rows name the same one
- nbr_index: int32 [256, 2], replicated, may hold values from 0 to 15
- depth_extent: int32 [256], P('tile'), may hold values from 16 to 256, as said below
Outputs:
- image: float32 [256, 8, 49, 256], P(('tile', 'tm'))
Inputs may be any that keep to these rules, and one draw needn't show every extreme that they name: `nbr_device`: the two devices of a row differ; among the rows of one device (aligned blocks of 16 rows) no device is named more than 3 times, and in some device's rows one device is named exactly 3 times. Cells of a tile's gathers at depth depth_extent[s] and below are zero.
All inputs are finite; a program needn't handle non-finite values.
Results may differ from a plain program's by a relative error of at most 0.0003.
Values may be sent and summed in bfloat16 or wider, within the bound.
No kernel may reach another device: no remote copies, remote signals or barrier semaphores. Data moves between devices by JAX's collectives and lax.ppermute only.
A program may use at most 128 MiB of HBM per device.

v0:
```python
import math

import jax
import jax.numpy as jnp
from jax import lax
from jax.sharding import PartitionSpec as P

GSTEP = 16
HMAX = 24
GB = 8
OFFS = 49
RIM_L = 16
RIM_R = 17


def window_stack(strip, first_cell, last_cell):
    begins = [RIM_L + GSTEP * gather + GSTEP // 2 - HMAX for gather in range(GB)]
    return jnp.stack(
        [strip[:, :, begin : begin + OFFS, first_cell:last_cell] for begin in begins], axis=2
    )


def correlate(src_part, rcv_part, weight, first_cell, last_cell):
    src_window = window_stack(src_part, first_cell, last_cell)[:, :, :, ::-1, :]
    rcv_window = window_stack(rcv_part, first_cell, last_cell)
    product = (
        src_window.astype(jnp.float32)
        * rcv_window.astype(jnp.float32)
        * weight[None, :, None, None, first_cell:last_cell]
    )
    return jnp.sum(product, axis=1)


def image_rows(src_part, rcv_part, weight, extent_part, norm_scale):
    depth_cells = src_part.shape[3]
    depth_index = jnp.arange(depth_cells, dtype=jnp.int32)
    total = correlate(src_part, rcv_part, weight, 0, depth_cells)
    depth_mask = (depth_index[None, :] < extent_part[:, None]).astype(jnp.float32)
    return total * norm_scale * depth_mask[:, None, None, :]


def local(src_snap, rcv_snap, q_rate, nbr_device, nbr_index, depth_extent):
    tile_count, step_count, block_width, depth_cells = src_snap.shape
    device_count = lax.axis_size("tile")
    own_index = lax.axis_index("tile")
    capacity = (2 * tile_count + device_count - 1) // device_count + 1
    request_count = 2 * tile_count
    wanted_device = nbr_device.reshape(device_count, request_count)
    wanted_index = nbr_index.reshape(device_count, request_count)
    named_here = (wanted_device == own_index).astype(jnp.int32)
    order_rank = jnp.cumsum(named_here, axis=1) - 1
    slot_ids = jnp.arange(capacity, dtype=jnp.int32)
    slot_hit = named_here[:, None, :] * (order_rank[:, None, :] == slot_ids[None, :, None]).astype(
        jnp.int32
    )
    send_index = jnp.sum(slot_hit * wanted_index[:, None, :], axis=2)
    flat_index = send_index.reshape(-1)
    mine_device = lax.dynamic_slice_in_dim(wanted_device, own_index, 1, 0)[0]
    request_ids = jnp.arange(request_count, dtype=jnp.int32)
    earlier = request_ids[:, None] > request_ids[None, :]
    same_source = (mine_device[:, None] == mine_device[None, :]) & earlier
    mine_rank = jnp.sum(same_source.astype(jnp.int32), axis=1)
    arrival = mine_device * capacity + mine_rank

    def pack_blocks(field):
        return jnp.take(field, flat_index, axis=0).reshape(
            device_count, capacity, step_count, block_width, depth_cells
        )

    incoming = (
        lax.all_to_all(pack_blocks(src_snap), "tile", split_axis=0, concat_axis=0, tiled=True),
        lax.all_to_all(pack_blocks(rcv_snap), "tile", split_axis=0, concat_axis=0, tiled=True),
    )

    def neighbours(received):
        stacked = received.reshape(device_count * capacity, step_count, block_width, depth_cells)
        fetched = jnp.take(stacked, arrival, axis=0).reshape(
            tile_count, 2, step_count, block_width, depth_cells
        )
        return (fetched[:, 0, :, block_width - RIM_L :, :], fetched[:, 1, :, :RIM_R, :])

    src_left, src_right = neighbours(incoming[0])
    rcv_left, rcv_right = neighbours(incoming[1])
    src_strip = jnp.concatenate([src_left, src_snap, src_right], axis=2)
    rcv_strip = jnp.concatenate([rcv_left, rcv_snap, rcv_right], axis=2)
    time_count = lax.axis_size("tm")
    total_steps = step_count * time_count
    norm_scale = 1.0 / math.sqrt(total_steps)
    time_steps = (
        lax.axis_index("tm") * step_count + jnp.arange(step_count, dtype=jnp.int32)
    ).astype(jnp.float32)
    weight = jnp.exp(q_rate[None, :] * time_steps[:, None] / total_steps)
    return lax.psum_scatter(
        image_rows(src_strip, rcv_strip, weight, depth_extent, norm_scale),
        "tm",
        scatter_dimension=0,
        tiled=True,
    )


def solution(mesh):
    placed = (P("tile", "tm", None, None), P("tile", "tm", None, None), P(), P(), P(), P("tile"))
    return jax.shard_map(
        local,
        mesh=mesh,
        in_specs=placed,
        out_specs=P(("tile", "tm"), None, None, None),
        check_vma=False,
    )
```

profile of v0, /device:TPU:2, one launch (start us, length us, event | category | flops | bytes accessed | tf_op | source)
XLA Modules:
  0.0 482.6 jit_solution(9288931429241991650)
XLA Ops:
  6.5 0.8 copy.12
  7.3 0.1 reshape.105
  7.5 0.2 reduce_window_sum.11
  7.7 0.8 copy.13
  8.5 0.1 mul.71
  8.6 0.1 multiply_reduce_fusion.1
  8.7 0.1 copy.14
  8.8 0.1 reshape.106
  9.0 0.0 copy-start
  9.0 6.7 %gather_fusion.2 = bf16[48,2,128,256]{3,2,1,0:T(8,128)(2,1)} fusion(bf16[16,2,128,256]{3,2,1,0:T(8,128)(2,1)} %param.11, s32[1024]{0:T(1024)S(1)} %pad_clamp_fusion.1), kind=kCustom, calls=%fused_computation.2.clone | custom fusion | bytes 12583104 | tf_op jit(solution)/shard_map/jit(_take)/gather | solution.py:66
  15.7 0.0 copy-done
  15.7 4.9 %gather_fusion = bf16[48,2,128,256]{3,2,1,0:T(8,128)(2,1)} fusion(bf16[16,2,128,256]{3,2,1,0:T(8,128)(2,1)S(1)} %copy-done, s32[1024]{0:T(1024)S(1)} %pad_clamp_fusion.1), kind=kCustom, calls=%fused_computation.clone | custom fusion | bytes 12583104 | tf_op jit(solution)/shard_map/jit(_take)/gather | solution.py:66
  20.6 8.4 %broadcast_select_fusion.1 = (bf16[48,2,128,256]{3,2,1,0:T(8,128)(2,1)}, bf16[48,2,128,256]{3,2,1,0:T(8,128)(2,1)S(1)}) fusion(bf16[48,2,128,256]{3,2,1,0:T(8,128)(2,1)} %gather_fusion, pred[48]{0:T(512)(128)(4,1)S(1)} %compare_and_fusion.1, bf16[48,2,128,256]{3,2,1,0:T(8,128)(2,1)} %gather_fusion.2), kind=kLoop, calls=%fused_computation.6 | loop fusion | flops 6291456 | bytes 25165872 | tf_op jit(solution)/shard_map/jit(_take)/select_n | solution.py:66
  28.9 148.0 %all_to_all.10 = bf16[16,3,2,128,256]{4,3,2,1,0:T(8,128)(2,1)} all-to-all(bf16[16,3,2,128,256]{4,3,2,1,0:T(8,128)(2,1)S(1)} %bitcast.64), channel_id=1, replica_groups=mesh['tile'=16,'tm'=16] {'tile'}, dimensions={0} | all-to-all | bytes 12582912 | tf_op jit(solution)/shard_map/all_to_all | solution.py:72
  177.0 4.8 all-to-all-start
  181.7 0.2 reduce-scatter.4.cloned.1.call-start
  182.0 0.2 convert_reduce_fusion
  182.2 0.0 copy-done.2
  182.2 0.1 multiply_exponential_fusion
  182.3 0.0 copy-done.3
  182.3 0.1 fusion.11
  182.4 5.6 %gather_fusion.3 = bf16[32,2,128,256]{3,2,1,0:T(8,128)(2,1)} fusion(bf16[48,2,128,256]{3,2,1,0:T(8,128)(2,1)} %bitcast.65, s32[1024]{0:T(1024)S(1)} %pad_clamp_fusion), kind=kCustom, calls=%fused_computation.3.clone | custom fusion | bytes 8388736 | tf_op jit(solution)/shard_map/jit(_take)/gather | solution.py:77
  188.0 132.9 %all-to-all-done = bf16[16,3,2,128,256]{4,3,2,1,0:T(8,128)(2,1)} async-done(((bf16[16,3,2,128,256]{4,3,2,1,0:T(8,128)(2,1)}), bf16[16,3,2,128,256]{4,3,2,1,0:T(8,128)(2,1)}, u32[]{:S(2)}, u32[]{:S(2)}) %all-to-all-start) | async-done | bytes 6291488 | tf_op jit(solution)/shard_map/all_to_all | solution.py:71
  320.9 5.6 %gather_fusion.1 = bf16[32,2,128,256]{3,2,1,0:T(8,128)(2,1)} fusion(bf16[48,2,128,256]{3,2,1,0:T(8,128)(2,1)} %bitcast.2, s32[1024]{0:T(1024)S(1)} %pad_clamp_fusion), kind=kCustom, calls=%fused_computation.1.clone | custom fusion | bytes 8388736 | tf_op jit(solution)/shard_map/jit(_take)/gather | solution.py:77
  326.5 3.9 broadcast_select_fusion.3
  330.6 1.0 fusion.9
  331.6 1.1 bitcast_dynamic-update-slice_fusion.9
  332.7 1.0 bitcast_dynamic-update-slice_fusion.8
  333.7 1.0 bitcast_dynamic-update-slice_fusion.7
  334.7 1.0 bitcast_dynamic-update-slice_fusion.6
  335.7 1.0 bitcast_dynamic-update-slice_fusion.5
  336.7 1.1 fusion.7
  337.8 1.0 fusion.6
  338.8 20.9 %rev.3 = bf16[16,2,8,49,256]{4,3,1,0,2:T(8,128)(2,1)} reverse(bf16[16,2,8,49,256]{4,3,1,0,2:T(8,128)(2,1)} %fusion.6), dimensions={3} | reverse | bytes 12845056 | tf_op jit(solution)/shard_map/rev | solution.py:24
  359.7 0.0 copy-done.1
  359.7 1.0 fusion.4
  360.7 1.0 bitcast_dynamic-update-slice_fusion.4
  361.8 1.0 bitcast_dynamic-update-slice_fusion.3
  362.8 1.0 bitcast_dynamic-update-slice_fusion.2
  363.8 1.0 bitcast_dynamic-update-slice_fusion.1
  364.8 1.0 bitcast_dynamic-update-slice_fusion
  365.8 1.0 fusion.2
  366.8 1.0 fusion.1
  367.8 11.6 %multiply_reduce_fusion = f32[16,8,49,256]{3,2,0,1:T(8,128)} fusion(bf16[16,2,8,49,256]{4,3,1,0,2:T(8,128)(2,1)} %fusion.1, bf16[16,2,8,49,256]{4,3,1,0,2:T(8,128)(2,1)} %rev.3, f32[2,256]{1,0:T(2,128)S(1)} %multiply_exponential_fusion), kind=kLoop, calls=%fused_computation.4 | loop fusion | flops 14450688 | bytes 19269632 | tf_op jit(solution)/shard_map/reduce_sum | solution.py:31
  379.4 3.8 broadcast_multiply_fusion
  383.3 6.4 %copy.15 = f32[16,8,49,256]{3,1,2,0:T(8,128)} copy(f32[16,8,49,256]{3,2,0,1:T(8,128)S(1)} %broadcast_multiply_fusion) | data formatting | bytes 12845056 | tf_op jit(solution)/shard_map/mul | solution.py:39
  389.7 0.0 reduce-scatter.4.cloned.1.call-update
  389.7 86.0 %reduce-scatter.4.cloned.1.call-done = f32[1,8,49,256]{3,1,2,0:T(8,128)} async-done(((f32[16,8,49,256]{3,1,2,0:T(8,128)}), f32[1,8,49,256]{3,1,2,0:T(8,128)}) %reduce-scatter.4.cloned.1.call-update) | async-done | bytes 401424
  (16 shorter events, 0.2 us)
Async XLA Ops:
  9.0 6.7 %copy-start = (bf16[16,2,128,256]{3,2,1,0:T(8,128)(2,1)S(1)}, bf16[16,2,128,256]{3,2,1,0:T(8,128)(2,1)}, u32[]{:S(2)}) copy-start(bf16[16,2,128,256]{3,2,1,0:T(8,128)(2,1)} %param.10) | copy-start | bytes 6291460
  177.0 5.3 %copy-start.2 = (f32[256]{0:T(256)S(1)}, f32[256]{0:T(256)}, u32[]{:S(2)}) copy-start(f32[256]{0:T(256)} %param.12) | copy-start | bytes 3076
  177.0 5.3 %copy-start.3 = (s32[16]{0:T(128)S(1)}, s32[16]{0:T(128)}, u32[]{:S(2)}) copy-start(s32[16]{0:T(128)} %param.15) | copy-start | bytes 196
  177.0 143.9 %all-to-all-start = ((bf16[16,3,2,128,256]{4,3,2,1,0:T(8,128)(2,1)}), bf16[16,3,2,128,256]{4,3,2,1,0:T(8,128)(2,1)}, u32[]{:S(2)}, u32[]{:S(2)}) async-start(bf16[16,3,2,128,256]{4,3,2,1,0:T(8,128)(2,1)} %bitcast.63), calls=%async_computation | async-start | bytes 12582912 | tf_op jit(solution)/shard_map/all_to_all | solution.py:71
  181.7 294.0 %reduce-scatter.4.cloned.1.call-start = ((), (), s32[]{:S(2)}) async-start(), calls=%async_computation.3 | async-start | bytes 6823936
  338.8 20.9 %copy-start.1 = (bf16[16,2,128,256]{3,2,1,0:T(8,128)(2,1)S(1)}, bf16[16,2,128,256]{3,2,1,0:T(8,128)(2,1)}, u32[]{:S(2)}) copy-start(bf16[16,2,128,256]{3,2,1,0:T(8,128)(2,1)} %param.11) | copy-start | bytes 6291460
Sparse Core Ops, SparseCore 0:
  389.9 85.8 reduce-scatter.3
where the time goes:
time: 483 us
  waiting for transfers between devices  219 us (45%)
  blocking collectives  148 us (31%)
  local copies, waits for them, and re-layouts  62.6 us (13%)
  other arithmetic  34.6 us (7%)
  between operations  13.6 us (3%)
  starting transfers between devices  4.98 us (1%)
    all_to_all x1, blocking collectives, local(): lax.all_to_all(pack_blocks(rcv_snap), 'tile', split_axis=0, concat_axis=0...  148 us
    all_to_all x1, waiting for transfers between devices, local(): lax.all_to_all(pack_blocks(src_snap), 'tile', split_axis=0, concat_axis=0...  133 us
    unnamed x2, waiting for transfers between devices  86 us
    rev x1, local copies, waits for them, and re-layouts, correlate(): src_window = window_stack(src_part, first_cell, last_cell)[:, :, :, ::-1, :]  20.9 us
    unnamed x20, local copies, waits for them, and re-layouts  11.8 us
    reduce_sum x1, other arithmetic, correlate(): return jnp.sum(product, axis=1)  11.6 us
    gather x2, local copies, waits for them, and re-layouts, pack_blocks(): jnp.take(field, flat_index, axis=0)  11.6 us
    gather x2, local copies, waits for them, and re-layouts, neighbours(): jnp.take(stacked, arrival, axis=0)  11.3 us
  transfers between devices with their start and end apart: 2, of which 2 were waited for; matrix products, arithmetic and copies ran while one was open for 1% of the time, Pallas kernels for 0%

commit v1 on v0

v1 whole, which is shorter than its diff:
```python
import functools
import math

import jax
import jax.numpy as jnp
from jax import lax
from jax.experimental import pallas as pl
from jax.experimental.pallas import tpu as pltpu
from jax.sharding import PartitionSpec as P

GSTEP = 16
GB = 8
OFFS = 49
RIM = 16
BODY = OFFS - 1


def pack_kernel(send_ref, src_lo, src_hi, rcv_lo, rcv_hi, out_ref, *, slots, steps):
    dest = pl.program_id(0)
    depth = out_ref.shape[2]
    tail = out_ref.shape[1] - slots * 2 * steps * RIM
    row_ids = lax.broadcasted_iota(jnp.int32, (tail, depth), 0)
    extra = jnp.zeros((tail, depth), jnp.float32)
    for slot in range(slots):
        choice = send_ref[dest * slots + slot]
        index = choice // 2
        right = choice % 2
        for field, (low, high) in enumerate(((src_lo, src_hi), (rcv_lo, rcv_hi))):
            for step in range(steps):
                at = (slot * 2 + field) * steps + step
                rows = low[index, step]
                rim = jnp.where(right == 1, rows[:RIM], high[index, step])
                out_ref[0, at * RIM : (at + 1) * RIM, :] = rim
                beyond = rows[RIM : RIM + 8].astype(jnp.float32)[0:1]
                extra = jnp.where(row_ids == at, beyond, extra)
    out_ref[0, slots * 2 * steps * RIM :, :] = extra.astype(out_ref.dtype)


def pack(send, src_snap, rcv_snap, slots):
    tiles, steps, width, depth = src_snap.shape
    devices = send.shape[0] // slots
    parts = slots * 2 * steps
    rows = parts * RIM + -(-parts // 16) * 16
    low = pl.BlockSpec((tiles, steps, RIM + 8, depth), lambda i, s: (0, 0, 0, 0))
    high = pl.BlockSpec((tiles, steps, RIM, depth), lambda i, s: (0, 0, width // RIM - 1, 0))
    return pl.pallas_call(
        functools.partial(pack_kernel, slots=slots, steps=steps),
        name="pack_rims",
        grid_spec=pltpu.PrefetchScalarGridSpec(
            num_scalar_prefetch=1,
            grid=(devices,),
            in_specs=[low, high, low, high],
            out_specs=pl.BlockSpec((1, rows, depth), lambda i, s: (i, 0, 0)),
        ),
        out_shape=jax.ShapeDtypeStruct((devices, rows, depth), src_snap.dtype),
    )(send, src_snap, src_snap, rcv_snap, rcv_snap)


def unpack_kernel(arrival_ref, in_ref, out_ref, *, slots, steps):
    tile = pl.program_id(0)
    rows = 2 * steps * RIM
    left = arrival_ref[2 * tile]
    right = arrival_ref[2 * tile + 1]
    left_device, left_slot = left // slots, left % slots
    right_device, right_slot = right // slots, right % slots
    out_ref[0, 0:rows, :] = in_ref[left_device, pl.ds(pl.multiple_of(left_slot * rows, 16), rows), :]
    out_ref[0, rows : 2 * rows, :] = in_ref[
        right_device, pl.ds(pl.multiple_of(right_slot * rows, 16), rows), :
    ]
    tail = in_ref[right_device, slots * rows :, :].astype(jnp.float32)
    count = 2 * steps
    picked = tail[0:count]
    for slot in range(1, slots):
        picked = jnp.where(right_slot == slot, tail[slot * count : (slot + 1) * count], picked)
    padded = jnp.concatenate([picked, jnp.zeros((8 - count, picked.shape[1]), jnp.float32)], axis=0)
    out_ref[0, 2 * rows :, :] = padded.astype(out_ref.dtype)


def unpack(arrival, received, slots, tiles, steps):
    devices, in_rows, depth = received.shape
    rows = 2 * (2 * steps * RIM) + 8
    return pl.pallas_call(
        functools.partial(unpack_kernel, slots=slots, steps=steps),
        name="unpack_rims",
        grid_spec=pltpu.PrefetchScalarGridSpec(
            num_scalar_prefetch=1,
            grid=(tiles,),
            in_specs=[pl.BlockSpec((devices, in_rows, depth), lambda i, s: (0, 0, 0))],
            out_specs=pl.BlockSpec((1, rows, depth), lambda i, s: (i, 0, 0)),
        ),
        out_shape=jax.ShapeDtypeStruct((tiles, rows, depth), received.dtype),
    )(arrival, received)


def image_kernel(
    extent_ref, q_ref, src_ref, rcv_ref, rim_ref, out_ref, rev_ref, fwd_ref, body_ref, last_ref, *, total_steps
):
    block = pl.program_id(0)
    parts, steps, width, depth = src_ref.shape
    strip = width + 2 * RIM
    rows = 2 * steps * RIM

    @pl.when(block == 0)
    def _():
        body_ref[...] = jnp.zeros_like(body_ref)
        last_ref[...] = jnp.zeros_like(last_ref)

    out_rows = rev_ref.shape[1]
    out_id = lax.broadcasted_iota(jnp.int32, (out_rows, strip), 0)
    in_id = lax.broadcasted_iota(jnp.int32, (out_rows, strip), 1)
    flip = (out_id <= strip) & (in_id == strip - out_id)
    pick = (out_id >= strip + 8) & (in_id == (out_id - (strip + 8)) * GSTEP)
    select = (flip | pick).astype(src_ref.dtype)

    end_out = lax.broadcasted_iota(jnp.int32, (GB, strip), 0)
    end_in = lax.broadcasted_iota(jnp.int32, (GB, strip), 1)
    end_pick = (end_in == end_out * GSTEP + BODY).astype(src_ref.dtype)
    end_id = lax.broadcasted_iota(jnp.int32, (GB, depth), 0)

    for part in range(parts):
        beyond = rim_ref[part, 2 * rows :, :].astype(jnp.float32)
        for step in range(steps):
            at = part * steps + step
            src_at, rcv_at = step * RIM, (steps + step) * RIM
            src_strip = jnp.concatenate(
                [
                    rim_ref[part, src_at : src_at + RIM, :],
                    src_ref[part, step],
                    rim_ref[part, rows + src_at : rows + src_at + RIM, :],
                ],
                axis=0,
            )
            rev_ref[at] = jnp.dot(select, src_strip, preferred_element_type=jnp.float32)
            rev_ref[at, 0:1, :] = beyond[step : step + 1]
            time = ((block * parts + part) * steps + step).astype(jnp.float32)
            weight = jnp.exp(q_ref[...] * time / total_steps)
            rcv_strip = jnp.concatenate(
                [
                    rim_ref[part, rcv_at : rcv_at + RIM, :],
                    rcv_ref[part, step],
                    rim_ref[part, rows + rcv_at : rows + rcv_at + RIM, :],
                ],
                axis=0,
            )
            fwd_ref[at, 0:strip, :] = rcv_strip.astype(jnp.float32) * weight
            ends = jnp.dot(end_pick, rcv_strip, preferred_element_type=jnp.float32)
            ends = jnp.where(end_id == GB - 1, beyond[steps + step : steps + step + 1], ends)
            fwd_ref[at, strip : strip + GB, :] = ends * weight

    many = parts * steps
    for gather in range(GB):
        rev_at = strip - BODY - GSTEP * gather
        fwd_at = GSTEP * gather
        total = body_ref[gather]
        for at in range(many):
            total += rev_ref[at, rev_at : rev_at + BODY, :] * fwd_ref[at, fwd_at : fwd_at + BODY, :]
        body_ref[gather] = total
    total = last_ref[...]
    for at in range(many):
        total += rev_ref[at, strip + 8 : strip + 16, :] * fwd_ref[at, strip : strip + GB, :]
    last_ref[...] = total

    @pl.when(block == pl.num_programs(0) - 1)
    def _():
        depth_id = lax.broadcasted_iota(jnp.int32, (1, depth), 1)
        scale = jnp.where(depth_id < extent_ref[0], 1.0, 0.0) * (1.0 / math.sqrt(total_steps))
        for gather in range(GB):
            out_ref[0, gather, 0:BODY, :] = body_ref[gather] * scale
            out_ref[0, gather, BODY:OFFS, :] = last_ref[gather : gather + 1, :] * scale


def image(extent, q_rate, src_all, rcv_all, rim_all):
    devices, steps, width, depth = src_all.shape
    parts = 2
    strip = width + 2 * RIM
    total_steps = devices * steps
    main = pl.BlockSpec((parts, steps, width, depth), lambda i, s: (i, 0, 0, 0))
    return pl.pallas_call(
        functools.partial(image_kernel, total_steps=total_steps),
        name="image_tile",
        grid_spec=pltpu.PrefetchScalarGridSpec(
            num_scalar_prefetch=1,
            grid=(devices // parts,),
            in_specs=[
                pl.BlockSpec((1, depth), lambda i, s: (0, 0)),
                main,
                main,
                pl.BlockSpec((parts, rim_all.shape[1], depth), lambda i, s: (i, 0, 0)),
            ],
            out_specs=pl.BlockSpec((1, GB, OFFS, depth), lambda i, s: (0, 0, 0, 0)),
            scratch_shapes=[
                pltpu.VMEM((parts * steps, strip + 16, depth), jnp.float32),
                pltpu.VMEM((parts * steps, strip + 8, depth), jnp.float32),
                pltpu.VMEM((GB, BODY, depth), jnp.float32),
                pltpu.VMEM((GB, depth), jnp.float32),
            ],
        ),
        out_shape=jax.ShapeDtypeStruct((1, GB, OFFS, depth), jnp.float32),
    )(extent, q_rate.reshape(1, depth), src_all, rcv_all, rim_all)


def routes(nbr_device, nbr_index, device_count, tile_count, slots, own_index):
    requests = 2 * tile_count
    device = nbr_device.reshape(device_count, requests)
    code = nbr_index.reshape(device_count, requests) * 2 + jnp.arange(requests, dtype=jnp.int32) % 2
    ids = jnp.arange(requests, dtype=jnp.int32)
    named = device == own_index
    rank = jnp.sum((named[:, None, :] & (ids[None, :] < ids[:, None])).astype(jnp.int32), axis=2)
    hit = named[:, None, :] & (rank[:, None, :] == jnp.arange(slots, dtype=jnp.int32)[None, :, None])
    send = jnp.sum(jnp.where(hit, code[:, None, :], 0), axis=2).reshape(-1)
    mine = lax.dynamic_slice_in_dim(device, own_index, 1, 0)[0]
    same = (mine[:, None] == mine[None, :]) & (ids[None, :] < ids[:, None])
    arrival = mine * slots + jnp.sum(same.astype(jnp.int32), axis=1)
    return send, arrival


def local(src_snap, rcv_snap, q_rate, nbr_device, nbr_index, depth_extent):
    tile_count, step_count, _, _ = src_snap.shape
    device_count = lax.axis_size("tile")
    slots = (2 * tile_count + device_count - 1) // device_count + 1
    send, arrival = routes(
        nbr_device, nbr_index, device_count, tile_count, slots, lax.axis_index("tile")
    )
    src_all = lax.all_to_all(src_snap, "tm", split_axis=0, concat_axis=0, tiled=True)
    rcv_all = lax.all_to_all(rcv_snap, "tm", split_axis=0, concat_axis=0, tiled=True)
    packed = pack(send, src_snap, rcv_snap, slots)
    received = lax.all_to_all(packed, "tile", split_axis=0, concat_axis=0, tiled=True)
    rims = unpack(arrival, received, slots, tile_count, step_count)
    rim_all = lax.all_to_all(rims, "tm", split_axis=0, concat_axis=0, tiled=True)
    extent = lax.dynamic_slice_in_dim(depth_extent, lax.axis_index("tm"), 1, 0)
    return image(extent, q_rate, src_all, rcv_all, rim_all)


def solution(mesh):
    placed = (P("tile", "tm", None, None), P("tile", "tm", None, None), P(), P(), P(), P("tile"))
    return jax.shard_map(
        local,
        mesh=mesh,
        in_specs=placed,
        out_specs=P(("tile", "tm"), None, None, None),
        check_vma=False,
    )
```

time: 483 us -> 159 us (0.33)
  waiting for transfers between devices: 219 us -> 55.7 us
  blocking collectives: 148 us -> 51.1 us
  local copies, waits for them, and re-layouts: 62.6 us -> 4.68 us
  other arithmetic: 34.6 us -> 1.22 us
  Pallas kernels: 0 us -> 22.3 us
  starting transfers between devices: 4.98 us -> 21.9 us
  between operations: 13.6 us -> 0.1 us
    all_to_all x1, blocking collectives: 148 us -> 51.1 us  [local(): lax.all_to_all(packed, 'tile', split_axis=0, concat_axis=0, tiled=True)]
    unnamed x2 -> x0, waiting for transfers between devices: 86 us -> none
    all_to_all x1 -> x3, waiting for transfers between devices: 133 us -> 55.7 us  [the longest x1 22.6 us: local(): lax.all_to_all(rcv_snap, 'tm', split_axis=0, concat_axis=0, tiled=True)]
    gather x4 -> x0, local copies, waits for them, and re-layouts: 22.9 us -> none  [the longest x2 11.6 us: pack_blocks(): jnp.take(field, flat_index, axis=0)]
    pallas_call x0 -> x3, Pallas kernels: none -> 22.3 us  [the longest x1 7.53 us: image(): pl.pallas_call(functools.partial(image_kernel, total_steps=total_steps),...]
    rev x1 -> x0, local copies, waits for them, and re-layouts: 20.9 us -> none  [correlate(): src_window = window_stack(src_part, first_cell, last_cell)[:, :, :, ::-1, :]]
    all_to_all x1 -> x3, starting transfers between devices: 4.76 us -> 21.9 us  [the longest x1 7.61 us: local(): lax.all_to_all(src_snap, 'tm', split_axis=0, concat_axis=0, tiled=True)]
    select_n x3 -> x1, other arithmetic: 12.3 us -> 0.01 us  [routes(): jnp.arange(requests, dtype=jnp.int32) % 2]
  transfers between devices with their start and end apart: 2 -> 3, of which waited for: 2 -> 3; matrix products, arithmetic and copies ran while one was open for 1% -> 2% of each run, Pallas kernels for 0% -> 9%
where the time goes in v1:
time: 159 us; the launch traced here: 157 us
  waiting for transfers between devices  55.7 us (35%)
  blocking collectives  51.1 us (32%)
  Pallas kernels  22.3 us (14%)
  starting transfers between devices  21.9 us (14%)
  local copies, waits for them, and re-layouts  4.68 us (3%)
    all_to_all x1, blocking collectives, local(): lax.all_to_all(packed, 'tile', split_axis=0, concat_axis=0, tiled=True)  51.1 us
    all_to_all x1, waiting for transfers between devices, local(): lax.all_to_all(rcv_snap, 'tm', split_axis=0, concat_axis=0, tiled=True)  22.6 us
    all_to_all x1, waiting for transfers between devices, local(): lax.all_to_all(src_snap, 'tm', split_axis=0, concat_axis=0, tiled=True)  18 us
    all_to_all x1, waiting for transfers between devices, local(): lax.all_to_all(rims, 'tm', split_axis=0, concat_axis=0, tiled=True)  15.1 us
    all_to_all x1, starting transfers between devices, local(): lax.all_to_all(src_snap, 'tm', split_axis=0, concat_axis=0, tiled=True)  7.61 us
    all_to_all x1, starting transfers between devices, local(): lax.all_to_all(rcv_snap, 'tm', split_axis=0, concat_axis=0, tiled=True)  7.56 us
    pallas_call x1, Pallas kernels, image(): pl.pallas_call(functools.partial(image_kernel, total_steps=total_steps),...  7.53 us
    pallas_call x1, Pallas kernels, unpack(): pl.pallas_call(functools.partial(unpack_kernel, slots=slots, steps=steps)...  7.42 us
  transfers between devices with their start and end apart: 3, of which 3 were waited for; matrix products, arithmetic and copies ran while one was open for 2% of the time, Pallas kernels for 9%

profile of v1, /device:TPU:2, one launch (start us, length us, event | category | flops | bytes accessed | tf_op | source)
XLA Modules:
  0.0 157.1 jit_solution(10940527019687210478)
XLA Ops:
  0.0 0.0 copy-start.2
  0.0 0.0 copy-start.3
  0.0 7.6 %all-to-all-start = ((bf16[16,2,128,256]{3,2,1,0:T(8,128)(2,1)}), bf16[16,2,128,256]{3,2,1,0:T(8,128)(2,1)S(1)}, u32[]{:S(2)}, u32[]{:S(2)}) async-start(bf16[16,2,128,256]{3,2,1,0:T(8,128)(2,1)} %src_hi.1), calls=%async_computation | async-start | bytes 4194304 | tf_op jit(solution)/shard_map/all_to_all | solution.py:224
  7.6 0.0 copy-done.2
  7.6 0.1 copy.11
  7.8 0.1 reshape.58
  7.9 0.0 copy-done.3
  7.9 0.1 copy.12
  8.0 0.1 mul.23
  8.2 0.3 convert_reduce_fusion
  8.6 0.1 select_reduce_fusion
  8.7 0.1 copy.13
  8.8 0.6 reshape.59.send_ref
  9.4 7.4 %pack_rims.1 = bf16[16,208,256]{2,1,0:T(8,128)(2,1)} custom-call(s32[48]{0:T(128)} %reshape.59.send_ref, bf16[16,2,128,256]{3,2,1,0:T(8,128)(2,1)} %src_hi.1, bf16[16,2,128,256]{3,2,1,0:T(8,128)(2,1)} %src_hi.1, bf16[16,2,128,256]{3,2,1,0:T(8,128)(2,1)} %rcv_hi.1, bf16[16,2,128,256]{3,2,1,0:T(8,128)(2,1)} %rcv_hi.1), custom_call_target="tpu_custom_call" | custom-call | tf_op jit(solution)/shard_map/pack_rims/pallas_call | solution.py:46
  16.8 18.0 %all-to-all-done.src_ref = bf16[16,2,128,256]{3,2,1,0:T(8,128)(2,1)S(1)} async-done(((bf16[16,2,128,256]{3,2,1,0:T(8,128)(2,1)}), bf16[16,2,128,256]{3,2,1,0:T(8,128)(2,1)S(1)}, u32[]{:S(2)}, u32[]{:S(2)}) %all-to-all-start) | async-done | bytes 2097184 | tf_op jit(solution)/shard_map/all_to_all | solution.py:224
  34.8 0.0 copy-start
  34.8 51.1 %all_to_all.20.in_ref = bf16[16,208,256]{2,1,0:T(8,128)(2,1)} all-to-all(bf16[16,208,256]{2,1,0:T(8,128)(2,1)} %pack_rims.1), channel_id=1, replica_groups=mesh['tile'=16,'tm'=16] {'tile'}, dimensions={0} | all-to-all | bytes 3407872 | tf_op jit(solution)/shard_map/all_to_all | solution.py:227
  85.9 0.0 copy-done
  85.9 7.6 %all-to-all-start.1 = ((bf16[16,2,128,256]{3,2,1,0:T(8,128)(2,1)}), bf16[16,2,128,256]{3,2,1,0:T(8,128)(2,1)}, u32[]{:S(2)}, u32[]{:S(2)}) async-start(bf16[16,2,128,256]{3,2,1,0:T(8,128)(2,1)} %rcv_hi.1), calls=%async_computation.1 | async-start | bytes 4194304 | tf_op jit(solution)/shard_map/all_to_all | solution.py:225
  93.5 0.2 convert_reduce_fusion.1
  93.6 0.5 multiply_add_fusion.arrival_ref
  94.2 0.0 copy-start.4
  94.2 7.4 %unpack_rims.1 = bf16[16,136,256]{2,1,0:T(8,128)(2,1)} custom-call(s32[32]{0:T(128)} %multiply_add_fusion.arrival_ref, bf16[16,208,256]{2,1,0:T(8,128)(2,1)} %all_to_all.20.in_ref), custom_call_target="tpu_custom_call" | custom-call | tf_op jit(solution)/shard_map/unpack_rims/pallas_call | solution.py:82
  101.6 22.6 %all-to-all-done.1.rcv_ref = bf16[16,2,128,256]{3,2,1,0:T(8,128)(2,1)} async-done(((bf16[16,2,128,256]{3,2,1,0:T(8,128)(2,1)}), bf16[16,2,128,256]{3,2,1,0:T(8,128)(2,1)}, u32[]{:S(2)}, u32[]{:S(2)}) %all-to-all-start.1) | async-done | bytes 2097184 | tf_op jit(solution)/shard_map/all_to_all | solution.py:225
  124.2 6.7 %all-to-all-start.3 = ((bf16[16,136,256]{2,1,0:T(8,128)(2,1)}), bf16[16,136,256]{2,1,0:T(8,128)(2,1)S(1)}, u32[]{:S(2)}, u32[]{:S(2)}) async-start(bf16[16,136,256]{2,1,0:T(8,128)(2,1)} %unpack_rims.1), calls=%async_computation.3 | async-start | bytes 2228224 | tf_op jit(solution)/shard_map/all_to_all | solution.py:229
  130.9 0.0 copy-done.4
  130.9 0.6 dynamic_slice.6.extent_ref
  131.5 15.1 %all-to-all-done.3.rim_ref = bf16[16,136,256]{2,1,0:T(8,128)(2,1)S(1)} async-done(((bf16[16,136,256]{2,1,0:T(8,128)(2,1)}), bf16[16,136,256]{2,1,0:T(8,128)(2,1)S(1)}, u32[]{:S(2)}, u32[]{:S(2)}) %all-to-all-start.3) | async-done | bytes 1114144 | tf_op jit(solution)/shard_map/all_to_all | solution.py:229
  146.7 0.0 copy-start.1
  146.7 1.0 copy-done.1
  147.7 7.5 %image_tile.1 = f32[1,8,49,256]{3,2,1,0:T(8,128)} custom-call(s32[1]{0:T(128)} %dynamic_slice.6.extent_ref, f32[1,256]{1,0:T(1,128)} %bitcast.5, bf16[16,2,128,256]{3,2,1,0:T(8,128)(2,1)} %copy-done, bf16[16,2,128,256]{3,2,1,0:T(8,128)(2,1)} %all-to-all-done.1.rcv_ref, bf16[16,136,256]{2,1,0:T(8,128)(2,1)} %copy-done.1), custom_call_target="tpu_custom_call" | custom-call | tf_op jit(solution)/shard_map/image_tile/pallas_call | solution.py:178
  155.2 1.9 %copy.14 = f32[1,8,49,256]{3,1,2,0:T(8,128)} copy(f32[1,8,49,256]{3,2,1,0:T(8,128)} %image_tile.1) | data formatting | bytes 802816 | tf_op jit(solution)/shard_map/image_tile/pallas_call | solution.py:178
  (6 shorter events, 0.0 us)
Async XLA Ops:
  0.0 7.6 %copy-start.2 = (s32[256,2]{0,1:T(2,128)S(1)}, s32[256,2]{0,1:T(2,128)}, u32[]{:S(2)}) copy-start(s32[256,2]{0,1:T(2,128)} %param.9) | copy-start | bytes 6148
  0.0 7.9 %copy-start.3 = (s32[256,2]{0,1:T(2,128)S(1)}, s32[256,2]{0,1:T(2,128)}, u32[]{:S(2)}) copy-start(s32[256,2]{0,1:T(2,128)} %param.10) | copy-start | bytes 6148
  0.0 34.8 %all-to-all-start = ((bf16[16,2,128,256]{3,2,1,0:T(8,128)(2,1)}), bf16[16,2,128,256]{3,2,1,0:T(8,128)(2,1)S(1)}, u32[]{:S(2)}, u32[]{:S(2)}) async-start(bf16[16,2,128,256]{3,2,1,0:T(8,128)(2,1)} %src_hi.1), calls=%async_computation | async-start | bytes 4194304 | tf_op jit(solution)/shard_map/all_to_all | solution.py:224
  34.8 51.1 %copy-start = (bf16[16,2,128,256]{3,2,1,0:T(8,128)(2,1)}, bf16[16,2,128,256]{3,2,1,0:T(8,128)(2,1)S(1)}, u32[]{:S(2)}) copy-start(bf16[16,2,128,256]{3,2,1,0:T(8,128)(2,1)S(1)} %all-to-all-done.src_ref) | copy-start | bytes 6291460
  85.9 38.3 %all-to-all-start.1 = ((bf16[16,2,128,256]{3,2,1,0:T(8,128)(2,1)}), bf16[16,2,128,256]{3,2,1,0:T(8,128)(2,1)}, u32[]{:S(2)}, u32[]{:S(2)}) async-start(bf16[16,2,128,256]{3,2,1,0:T(8,128)(2,1)} %rcv_hi.1), calls=%async_computation.1 | async-start | bytes 4194304 | tf_op jit(solution)/shard_map/all_to_all | solution.py:225
  94.2 36.8 %copy-start.4 = (s32[16]{0:T(128)S(1)}, s32[16]{0:T(128)}, u32[]{:S(2)}) copy-start(s32[16]{0:T(128)} %param.11) | copy-start | bytes 196
  124.2 22.5 %all-to-all-start.3 = ((bf16[16,136,256]{2,1,0:T(8,128)(2,1)}), bf16[16,136,256]{2,1,0:T(8,128)(2,1)S(1)}, u32[]{:S(2)}, u32[]{:S(2)}) async-start(bf16[16,136,256]{2,1,0:T(8,128)(2,1)} %unpack_rims.1), calls=%async_computation.3 | async-start | bytes 2228224 | tf_op jit(solution)/shard_map/all_to_all | solution.py:229
  146.7 1.0 copy-start.1

commit v2 on v0

v2 whole, which is shorter than its diff:
```python
import functools
import math

import jax
import jax.numpy as jnp
from jax import lax
from jax.experimental import pallas as pl
from jax.experimental.pallas import tpu as pltpu
from jax.sharding import PartitionSpec as P

GSTEP = 16
GB = 8
OFFS = 49
RIM = 16
BODY = OFFS - 1


def pack_kernel(send_ref, dest_ref, src_lo, src_hi, rcv_lo, rcv_hi, *out_refs, slots, steps):
    tail = out_refs[0].shape[0] - slots * 2 * steps * RIM
    depth = out_refs[0].shape[1]
    row_ids = lax.broadcasted_iota(jnp.int32, (tail, depth), 0)
    for shift, out_ref in enumerate(out_refs):
        dest = dest_ref[shift]
        extra = jnp.zeros((tail, depth), jnp.float32)
        for slot in range(slots):
            choice = send_ref[dest * slots + slot]
            index = choice // 2
            right = choice % 2
            for field, (low, high) in enumerate(((src_lo, src_hi), (rcv_lo, rcv_hi))):
                for step in range(steps):
                    at = (slot * 2 + field) * steps + step
                    rows = low[index, step]
                    rim = jnp.where(right == 1, rows[:RIM], high[index, step])
                    out_ref[at * RIM : (at + 1) * RIM, :] = rim
                    beyond = rows[RIM : RIM + 8].astype(jnp.float32)[0:1]
                    extra = jnp.where(row_ids == at, beyond, extra)
        out_ref[slots * 2 * steps * RIM :, :] = extra.astype(out_ref.dtype)


def pack(send, dest, src_snap, rcv_snap, slots):
    tiles, steps, width, depth = src_snap.shape
    devices = dest.shape[0]
    parts = slots * 2 * steps
    rows = parts * RIM + -(-parts // 16) * 16
    low = pl.BlockSpec((tiles, steps, RIM + 8, depth), lambda i, s, d: (0, 0, 0, 0))
    high = pl.BlockSpec((tiles, steps, RIM, depth), lambda i, s, d: (0, 0, width // RIM - 1, 0))
    return pl.pallas_call(
        functools.partial(pack_kernel, slots=slots, steps=steps),
        name="pack_rims",
        grid_spec=pltpu.PrefetchScalarGridSpec(
            num_scalar_prefetch=2,
            grid=(1,),
            in_specs=[low, high, low, high],
            out_specs=[pl.BlockSpec((rows, depth), lambda i, s, d: (0, 0))] * devices,
        ),
        out_shape=[jax.ShapeDtypeStruct((rows, depth), src_snap.dtype)] * devices,
    )(send, dest, src_snap, src_snap, rcv_snap, rcv_snap)


def unpack_kernel(arrival_ref, *refs, devices, slots, steps):
    in_refs, out_ref, all_ref = refs[:devices], refs[-2], refs[-1]
    for device, in_ref in enumerate(in_refs):
        all_ref[device] = in_ref[...]
    rows = 2 * steps * RIM
    count = 2 * steps
    for tile in range(out_ref.shape[0]):
        left = arrival_ref[2 * tile]
        right = arrival_ref[2 * tile + 1]
        left_device, left_slot = left // slots, left % slots
        right_device, right_slot = right // slots, right % slots
        out_ref[tile, 0:rows, :] = all_ref[left_device, pl.ds(pl.multiple_of(left_slot * rows, 16), rows), :]
        out_ref[tile, rows : 2 * rows, :] = all_ref[
            right_device, pl.ds(pl.multiple_of(right_slot * rows, 16), rows), :
        ]
        tail = all_ref[right_device, slots * rows :, :].astype(jnp.float32)
        picked = tail[0:count]
        for slot in range(1, slots):
            picked = jnp.where(right_slot == slot, tail[slot * count : (slot + 1) * count], picked)
        first = [
            out_ref[tile, rows + at * RIM : rows + at * RIM + 8, :].astype(jnp.float32)[0:1]
            for at in range(count)
        ]
        out_ref[tile, 2 * rows :, :] = jnp.concatenate([picked, *first], axis=0).astype(out_ref.dtype)


def unpack(arrival, received, slots, tiles, steps):
    devices = len(received)
    in_rows, depth = received[0].shape
    dtype = received[0].dtype
    rows = 2 * (2 * steps * RIM) + 4 * steps
    return pl.pallas_call(
        functools.partial(unpack_kernel, devices=devices, slots=slots, steps=steps),
        name="unpack_rims",
        grid_spec=pltpu.PrefetchScalarGridSpec(
            num_scalar_prefetch=1,
            grid=(1,),
            in_specs=[pl.BlockSpec((in_rows, depth), lambda i, s: (0, 0))] * devices,
            out_specs=pl.BlockSpec((tiles, rows, depth), lambda i, s: (0, 0, 0)),
            scratch_shapes=[pltpu.VMEM((devices, in_rows, depth), dtype)],
        ),
        out_shape=jax.ShapeDtypeStruct((tiles, rows, depth), dtype),
    )(arrival, *received)


def inner_kernel(
    q_ref, main_ref, out_ref, side_ref, rev_ref, fwd_ref, body_ref, last_ref, *, total_steps, parts
):
    devices, fields, width, _ = main_ref.shape
    steps = fields // 2
    strip = width + 2 * RIM
    rows = 2 * steps * RIM
    many = parts * steps
    body_ref[...] = jnp.zeros_like(body_ref)
    last_ref[...] = jnp.zeros_like(last_ref)
    fwd_ref[...] = jnp.zeros_like(fwd_ref)

    out_rows = rev_ref.shape[1]
    out_id = lax.broadcasted_iota(jnp.int32, (out_rows, width), 0)
    in_id = lax.broadcasted_iota(jnp.int32, (out_rows, width), 1) + RIM
    flip = (out_id <= strip) & (in_id == strip - out_id)
    pick = (out_id >= strip + 8) & (in_id == (out_id - (strip + 8)) * GSTEP)
    select = (flip | pick).astype(main_ref.dtype)
    pick_rows = 2 * RIM + 2 * 8
    row = lax.broadcasted_iota(jnp.int32, (pick_rows, width), 0)
    cell = lax.broadcasted_iota(jnp.int32, (pick_rows, width), 1)
    meet = jnp.where(row < RIM, 2 * RIM - row, width - row)
    meet = jnp.where(row == 2 * RIM, width - 2 * RIM, meet)
    meet = jnp.where(row == 2 * RIM + 1, width - 3 * RIM, meet)
    ends = (row - (2 * RIM + 8)) * GSTEP + BODY - RIM
    meet = jnp.where(row >= 2 * RIM + 8, ends, meet)
    side_pick = (cell == meet).astype(main_ref.dtype)

    def block(number, carry):
        for part in range(parts):
            source = number * parts + part
            for step in range(steps):
                at = part * steps + step
                time = (source * steps + step).astype(jnp.float32)
                weight = jnp.exp(q_ref[...] * time / total_steps)
                own_src = main_ref[source, step]
                own_rcv = main_ref[source, steps + step]
                rev_ref[at] = jnp.dot(select, own_src, preferred_element_type=jnp.float32)
                fwd_ref[at, RIM : RIM + width, :] = own_rcv.astype(jnp.float32) * weight
                for group, own in enumerate((own_rcv, own_src)):
                    chosen = jnp.dot(side_pick, own, preferred_element_type=jnp.float32) * weight
                    low = (group * steps + step) * RIM
                    one = group * steps + step
                    side_ref[source, low : low + RIM, :] = chosen[0:RIM]
                    side_ref[source, rows + low : rows + low + RIM, :] = chosen[RIM : 2 * RIM]
                    side_ref[source, 2 * rows + one : 2 * rows + one + 1, :] = chosen[2 * RIM : 2 * RIM + 1]
                    one += 2 * rows + 2 * steps
                    side_ref[source, one : one + 1, :] = chosen[2 * RIM + 1 : 2 * RIM + 2]
                    if group == 0:
                        fwd_ref[at, strip + 8 : strip + 16, :] = chosen[2 * RIM + 8 :]
        for gather in range(GB):
            rev_at = strip - BODY - GSTEP * gather
            fwd_at = GSTEP * gather
            total = body_ref[gather]
            for at in range(many):
                total += rev_ref[at, rev_at : rev_at + BODY, :] * fwd_ref[at, fwd_at : fwd_at + BODY, :]
            body_ref[gather] = total
        total = last_ref[...]
        for at in range(many):
            total += rev_ref[at, strip + 8 : strip + 16, :] * fwd_ref[at, strip + 8 : strip + 16, :]
        last_ref[...] = total
        return carry

    lax.fori_loop(0, devices // parts, block, 0)
    for gather in range(GB):
        out_ref[0:BODY, gather, :] = body_ref[gather]
    out_ref[BODY, :, :] = last_ref[...]


def inner(q_rate, both):
    devices, fields, width, depth = both.shape
    steps = fields // 2
    parts = 2
    strip = width + 2 * RIM
    side_rows = 4 * steps * RIM + 4 * steps
    return pl.pallas_call(
        functools.partial(inner_kernel, total_steps=devices * steps, parts=parts),
        name="inner_cells",
        grid=(1,),
        in_specs=[
            pl.BlockSpec((1, depth), lambda i: (0, 0)),
            pl.BlockSpec(both.shape, lambda i: (0, 0, 0, 0)),
        ],
        out_specs=[
            pl.BlockSpec((OFFS, GB, depth), lambda i: (0, 0, 0)),
            pl.BlockSpec((devices, side_rows, depth), lambda i: (0, 0, 0)),
        ],
        scratch_shapes=[
            pltpu.VMEM((parts * steps, strip + 16, depth), jnp.float32),
            pltpu.VMEM((parts * steps, strip + 16, depth), jnp.float32),
            pltpu.VMEM((GB, BODY, depth), jnp.float32),
            pltpu.VMEM((GB, depth), jnp.float32),
        ],
        out_shape=[
            jax.ShapeDtypeStruct((OFFS, GB, depth), jnp.float32),
            jax.ShapeDtypeStruct((devices, side_rows, depth), jnp.float32),
        ],
    )(q_rate.reshape(1, depth), both)


def outer_kernel(extent_ref, in_ref, side_ref, rim_ref, out_ref, *, steps, norm):
    devices, side_rows, depth = side_ref.shape
    rows = 2 * steps * RIM
    depth_id = lax.broadcasted_iota(jnp.int32, (1, depth), 1)
    scale = jnp.where(depth_id < extent_ref[0], norm, 0.0)
    out_ref[...] = in_ref[...] * scale

    def total(low, high):
        kept = jnp.zeros((high - low, depth), jnp.float32)
        for device in range(devices):
            kept += side_ref[device, low:high, :] * rim_ref[device, low:high, :].astype(jnp.float32)
        return kept * scale

    def put(offset, gather, value):
        out_ref[offset, gather : gather + 1, :] += value

    width_steps = steps * RIM
    for base, gather, falls, rises in ((0, 0, BODY, 0), (rows, GB - 1, RIM, 2 * RIM)):
        for field in range(2):
            found = total(base + field * width_steps, base + (field + 1) * width_steps)
            found = sum(found[step * RIM : (step + 1) * RIM] for step in range(steps))
            for cell in range(RIM):
                put(falls - cell if field == 0 else rises + cell, gather, found[cell : cell + 1])
    found = total(2 * rows, side_rows)
    for one, (offset, gather) in enumerate(((0, GB - 1), (BODY, GB - 1), (0, GB - 2), (BODY, GB - 2))):
        low = one * steps
        put(offset, gather, sum(found[low + step : low + step + 1] for step in range(steps)))


def outer(extent, part, side, rims):
    devices, side_rows, _ = side.shape
    steps = side_rows // (4 * RIM + 4)
    by_offset = pl.pallas_call(
        functools.partial(outer_kernel, steps=steps, norm=1.0 / math.sqrt(devices * steps)),
        name="rim_cells",
        grid_spec=pltpu.PrefetchScalarGridSpec(
            num_scalar_prefetch=1,
            grid=(1,),
            in_specs=[
                pl.BlockSpec(part.shape, lambda i, s: (0, 0, 0)),
                pl.BlockSpec(side.shape, lambda i, s: (0, 0, 0)),
                pl.BlockSpec(rims.shape, lambda i, s: (0, 0, 0)),
            ],
            out_specs=pl.BlockSpec(part.shape, lambda i, s: (0, 0, 0)),
        ),
        out_shape=jax.ShapeDtypeStruct(part.shape, part.dtype),
    )(extent, part, side, rims)
    return by_offset.transpose(1, 0, 2)[None]


def routes(nbr_device, nbr_index, device_count, tile_count, slots, own_index):
    requests = 2 * tile_count
    device = nbr_device.reshape(device_count, requests)
    code = nbr_index.reshape(device_count, requests) * 2 + jnp.arange(requests, dtype=jnp.int32) % 2
    ids = jnp.arange(requests, dtype=jnp.int32)
    named = device == own_index
    rank = jnp.sum((named[:, None, :] & (ids[None, :] < ids[:, None])).astype(jnp.int32), axis=2)
    hit = named[:, None, :] & (rank[:, None, :] == jnp.arange(slots, dtype=jnp.int32)[None, :, None])
    send = jnp.sum(jnp.where(hit, code[:, None, :], 0), axis=2).reshape(-1)
    mine = lax.dynamic_slice_in_dim(device, own_index, 1, 0)[0]
    same = (mine[:, None] == mine[None, :]) & (ids[None, :] < ids[:, None])
    rank_here = jnp.sum(same.astype(jnp.int32), axis=1)
    return send, mine, rank_here


def local(src_snap, rcv_snap, q_rate, nbr_device, nbr_index, depth_extent):
    tile_count, step_count, _, _ = src_snap.shape
    device_count = lax.axis_size("tile")
    slots = (2 * tile_count + device_count - 1) // device_count + 1
    own = lax.axis_index("tile")
    send, mine, rank_here = routes(nbr_device, nbr_index, device_count, tile_count, slots, own)

    count = device_count // 2
    moves = [(major, minor) for major in range(count) for minor in range(2)]
    ids = jnp.arange(device_count, dtype=jnp.int32)
    dest = (own // 2 + ids // 2) % count * 2 + (own % 2 + ids % 2) % 2
    arrival = ((own // 2 - mine // 2) % count * 2 + (own % 2 - mine % 2) % 2) * slots + rank_here

    both = jnp.concatenate([src_snap, rcv_snap], axis=1)
    both = lax.all_to_all(both, "tm", split_axis=0, concat_axis=0, tiled=True)
    packed = pack(send, dest, src_snap, rcv_snap, slots)
    received = [packed[0]]
    for piece, (major, minor) in zip(packed[1:], moves[1:]):
        pairs = [
            (high * 2 + low, (high + major) % count * 2 + (low + minor) % 2)
            for high in range(count)
            for low in range(2)
        ]
        received.append(lax.ppermute(piece, "tile", pairs))
    rims = unpack(arrival, received, slots, tile_count, step_count)
    rim_all = lax.all_to_all(rims, "tm", split_axis=0, concat_axis=0, tiled=True)
    part, side = inner(q_rate, both)
    extent = lax.dynamic_slice_in_dim(depth_extent, lax.axis_index("tm"), 1, 0)
    return outer(extent, part, side, rim_all)


def solution(mesh):
    placed = (P("tile", "tm", None, None), P("tile", "tm", None, None), P(), P(), P(), P("tile"))
    return jax.shard_map(
        local,
        mesh=mesh,
        in_specs=placed,
        out_specs=P(("tile", "tm"), None, None, None),
        check_vma=False,
    )
```

time: 483 us -> 111 us (0.23)
  the two profiles are of different devices: /device:TPU:2 before, /device:TPU:32 now
where the time goes in v2:
time: 111 us
  starting transfers between devices  45.2 us (41%)
  waiting for transfers between devices  38 us (34%)
  Pallas kernels  17.4 us (16%)
  other arithmetic  6.49 us (6%)
  local copies, waits for them, and re-layouts  3.38 us (3%)
    ppermute x15, starting transfers between devices, local(): received.append(lax.ppermute(piece, 'tile', pairs))  30.4 us
    ppermute x15, waiting for transfers between devices, local(): received.append(lax.ppermute(piece, 'tile', pairs))  26.3 us
    all_to_all x1, waiting for transfers between devices, local(): lax.all_to_all(rims, 'tm', split_axis=0, concat_axis=0, tiled=True)  11.7 us
    all_to_all x1, starting transfers between devices, local(): lax.all_to_all(rims, 'tm', split_axis=0, concat_axis=0, tiled=True)  7.61 us
    all_to_all x1, starting transfers between devices, local(): both = lax.all_to_all(both, 'tm', split_axis=0, concat_axis=0, tiled=True)  7.22 us
    pallas_call x1, Pallas kernels, inner(): pl.pallas_call(functools.partial(inner_kernel, total_steps=devices * step...  6.49 us
    concatenate x1, other arithmetic, local(): both = jnp.concatenate([src_snap, rcv_snap], axis=1)  4.6 us
    pallas_call x1, Pallas kernels, unpack(): pl.pallas_call(functools.partial(unpack_kernel, devices=devices, slots=sl...  3.69 us
  transfers between devices with their start and end apart: 17, of which 8 were waited for; matrix products, arithmetic and copies ran while one was open for 3% of the time, Pallas kernels for 12%

profile of v2, /device:TPU:32, one launch (start us, length us, event | category | flops | bytes accessed | tf_op | source)
XLA Modules:
  0.0 110.8 jit_solution(5583702623914151730)
XLA Ops:
  0.0 4.6 %pad_maximum_fusion = bf16[16,4,128,256]{3,2,1,0:T(8,128)(2,1)} fusion(bf16[16,2,128,256]{3,2,1,0:T(8,128)(2,1)} %rcv_hi.1, bf16[16,2,128,256]{3,2,1,0:T(8,128)(2,1)} %src_hi.1), kind=kLoop, calls=%fused_computation | loop fusion | flops 2097152 | bytes 8388608 | tf_op jit(solution)/shard_map/concatenate | solution.py:283
  4.6 7.2 %all-to-all-start = ((bf16[16,4,128,256]{3,2,1,0:T(8,128)(2,1)}), bf16[16,4,128,256]{3,2,1,0:T(8,128)(2,1)}, u32[]{:S(2)}, u32[]{:S(2)}) async-start(bf16[16,4,128,256]{3,2,1,0:T(8,128)(2,1)} %pad_maximum_fusion), calls=%async_computation | async-start | bytes 8388608 | tf_op jit(solution)/shard_map/all_to_all | solution.py:284
  11.9 0.1 copy.9
  12.0 0.1 reshape.58
  12.1 0.1 copy.10
  12.3 0.1 mul.31
  12.4 0.3 convert_reduce_fusion
  12.8 0.1 select_reduce_fusion
  12.9 0.1 copy.11
  13.0 0.6 reshape.59.send_ref
  13.6 0.5 fusion.3.dest_ref
  14.2 3.6 %pack_rims.1 = (bf16[208,256]{1,0:T(8,128)(2,1)}, bf16[208,256]{1,0:T(8,128)(2,1)}, bf16[208,256]{1,0:T(8,128)(2,1)}, bf16[208,256]{1,0:T(8,128)(2,1)}, bf16[208...) custom-call(s32[48]{0:T(128)} %reshape.59.send_ref, ...), custom_call_target="tpu_custom_call" | custom-call | tf_op jit(solution)/shard_map/pack_rims/pallas_call | solution.py:47
  17.8 0.0 collective-permute-start
  17.8 2.0 %collective-permute-start.1 = (bf16[208,256]{1,0:T(8,128)(2,1)}, bf16[208,256]{1,0:T(8,128)(2,1)S(1)}, u32[]{:S(2)}, u32[]{:S(2)}) collective-permute-start(bf16[208,256]{1,0:T(8,128)(2,1)} %get-tuple-element.27), channel_id=1, source_target_pairs={{0,32},{16,48},{32,64},{48,80},{64,96},{80,112},{96,128},{112,144}... | collective-permute-start | bytes 319496 | tf_op jit(solution)/shard_map/ppermute | solution.py:293
  19.8 1.7 %collective-permute-start.2 = (bf16[208,256]{1,0:T(8,128)(2,1)}, bf16[208,256]{1,0:T(8,128)(2,1)S(1)}, u32[]{:S(2)}, u32[]{:S(2)}) collective-permute-start(bf16[208,256]{1,0:T(8,128)(2,1)} %get-tuple-element.28), channel_id=1, source_target_pairs={{0,48},{16,32},{32,80},{48,64},{64,112},{80,96},{96,144},{112,128}... | collective-permute-start | bytes 319496 | tf_op jit(solution)/shard_map/ppermute | solution.py:293
  21.4 3.6 %collective-permute-start.3 = (bf16[208,256]{1,0:T(8,128)(2,1)}, bf16[208,256]{1,0:T(8,128)(2,1)S(1)}, u32[]{:S(2)}, u32[]{:S(2)}) collective-permute-start(bf16[208,256]{1,0:T(8,128)(2,1)} %get-tuple-element.29), channel_id=1, source_target_pairs={{0,64},{16,80},{32,96},{48,112},{64,128},{80,144},{96,160},{112,17... | collective-permute-start | bytes 319496 | tf_op jit(solution)/shard_map/ppermute | solution.py:293
  25.0 1.2 %collective-permute-start.4 = (bf16[208,256]{1,0:T(8,128)(2,1)}, bf16[208,256]{1,0:T(8,128)(2,1)S(1)}, u32[]{:S(2)}, u32[]{:S(2)}) collective-permute-start(bf16[208,256]{1,0:T(8,128)(2,1)} %get-tuple-element.30), channel_id=1, source_target_pairs={{0,80},{16,64},{32,112},{48,96},{64,144},{80,128},{96,176},{112,16... | collective-permute-start | bytes 319496 | tf_op jit(solution)/shard_map/ppermute | solution.py:293
  26.2 0.0 collective-permute-done.refs_1_
  26.2 0.2 collective-permute-start.5
  26.4 0.0 collective-permute-done.1.refs_2_
  26.4 4.7 %collective-permute-start.6 = (bf16[208,256]{1,0:T(8,128)(2,1)}, bf16[208,256]{1,0:T(8,128)(2,1)S(1)}, u32[]{:S(2)}, u32[]{:S(2)}) collective-permute-start(bf16[208,256]{1,0:T(8,128)(2,1)} %get-tuple-element.32), channel_id=1, source_target_pairs={{0,112},{16,96},{32,144},{48,128},{64,176},{80,160},{96,208},{112,... | collective-permute-start | bytes 319496 | tf_op jit(solution)/shard_map/ppermute | solution.py:293
  31.1 0.0 collective-permute-done.2.refs_3_
  31.1 0.9 collective-permute-start.7
  32.0 3.8 %collective-permute-done.3.refs_4_ = bf16[208,256]{1,0:T(8,128)(2,1)S(1)} collective-permute-done((bf16[208,256]{1,0:T(8,128)(2,1)}, bf16[208,256]{1,0:T(8,128)(2,1)S(1)}, u32[]{:S(2)}, u32[]{:S(2)}) %collective-permute-start.3) | collective-permute-done | bytes 106528 | tf_op jit(solution)/shard_map/ppermute | solution.py:293
  35.8 3.0 %collective-permute-start.8 = (bf16[208,256]{1,0:T(8,128)(2,1)}, bf16[208,256]{1,0:T(8,128)(2,1)S(1)}, u32[]{:S(2)}, u32[]{:S(2)}) collective-permute-start(bf16[208,256]{1,0:T(8,128)(2,1)} %get-tuple-element.34), channel_id=1, source_target_pairs={{0,144},{16,128},{32,176},{48,160},{64,208},{80,192},{96,240},{112... | collective-permute-start | bytes 319496 | tf_op jit(solution)/shard_map/ppermute | solution.py:293
  38.7 0.0 collective-permute-done.4.refs_5_
  38.7 0.0 collective-permute-start.9
  38.7 0.2 convert_reduce_fusion.1
  38.9 11.2 %collective-permute-done.5.refs_6_ = bf16[208,256]{1,0:T(8,128)(2,1)S(1)} collective-permute-done((bf16[208,256]{1,0:T(8,128)(2,1)}, bf16[208,256]{1,0:T(8,128)(2,1)S(1)}, u32[]{:S(2)}, u32[]{:S(2)}) %collective-permute-start.5) | collective-permute-done | bytes 106528 | tf_op jit(solution)/shard_map/ppermute | solution.py:293
  50.2 0.0 collective-permute-start.10
  50.2 2.6 %collective-permute-done.6.refs_7_ = bf16[208,256]{1,0:T(8,128)(2,1)S(1)} collective-permute-done((bf16[208,256]{1,0:T(8,128)(2,1)}, bf16[208,256]{1,0:T(8,128)(2,1)S(1)}, u32[]{:S(2)}, u32[]{:S(2)}) %collective-permute-start.6) | collective-permute-done | bytes 106528 | tf_op jit(solution)/shard_map/ppermute | solution.py:293
  52.8 7.7 %collective-permute-start.12 = (bf16[208,256]{1,0:T(8,128)(2,1)}, bf16[208,256]{1,0:T(8,128)(2,1)S(1)}, u32[]{:S(2)}, u32[]{:S(2)}) collective-permute-start(bf16[208,256]{1,0:T(8,128)(2,1)} %get-tuple-element.38), channel_id=1, source_target_pairs={{0,208},{16,192},{32,240},{48,224},{64,16},{80,0},{96,48},{112,32}... | collective-permute-start | bytes 319496 | tf_op jit(solution)/shard_map/ppermute | solution.py:293
  60.5 5.5 %collective-permute-start.13 = (bf16[208,256]{1,0:T(8,128)(2,1)}, bf16[208,256]{1,0:T(8,128)(2,1)S(1)}, u32[]{:S(2)}, u32[]{:S(2)}) collective-permute-start(bf16[208,256]{1,0:T(8,128)(2,1)} %get-tuple-element.39), channel_id=1, source_target_pairs={{0,224},{16,240},{32,0},{48,16},{64,32},{80,48},{96,64},{112,80},{... | collective-permute-start | bytes 319496 | tf_op jit(solution)/shard_map/ppermute | solution.py:293
  66.0 0.0 collective-permute-done.9.refs_10_
  66.0 0.0 collective-permute-start.14
  66.1 0.6 multiply_add_fusion.arrival_ref
  66.7 0.4 collective-permute-done.11.refs_12_
  67.1 1.3 %collective-permute-done.12.refs_13_ = bf16[208,256]{1,0:T(8,128)(2,1)S(1)} collective-permute-done((bf16[208,256]{1,0:T(8,128)(2,1)}, bf16[208,256]{1,0:T(8,128)(2,1)S(1)}, u32[]{:S(2)}, u32[]{:S(2)}) %collective-permute-start.12) | collective-permute-done | bytes 106528 | tf_op jit(solution)/shard_map/ppermute | solution.py:293
  68.4 5.4 %collective-permute-done.13.refs_14_ = bf16[208,256]{1,0:T(8,128)(2,1)S(1)} collective-permute-done((bf16[208,256]{1,0:T(8,128)(2,1)}, bf16[208,256]{1,0:T(8,128)(2,1)S(1)}, u32[]{:S(2)}, u32[]{:S(2)}) %collective-permute-start.13) | collective-permute-done | bytes 106528 | tf_op jit(solution)/shard_map/ppermute | solution.py:293
  73.8 1.5 %collective-permute-done.14.refs_15_ = bf16[208,256]{1,0:T(8,128)(2,1)S(1)} collective-permute-done((bf16[208,256]{1,0:T(8,128)(2,1)}, bf16[208,256]{1,0:T(8,128)(2,1)S(1)}, u32[]{:S(2)}, u32[]{:S(2)}) %collective-permute-start.14) | collective-permute-done | bytes 106528 | tf_op jit(solution)/shard_map/ppermute | solution.py:293
  75.5 0.5 copy-done.15
  76.0 3.7 %unpack_rims.1 = bf16[16,136,256]{2,1,0:T(8,128)(2,1)} custom-call(s32[32]{0:T(128)} %multiply_add_fusion.arrival_ref, bf16[208,256]{1,0:T(8,128)(2,1)} %get-tuple-element.25.refs_0_, bf16[208,256]{1,0:T(8,128)(2,1)} %copy-done.1, bf16[208,256]{1,0:T(8,128)(2,1)} %copy-done.2, bf16[208,256]{1,0:T(8,128)(2,1)} %copy-done.3, bf16[208,256]{1,0:T(8,128)(2,1)} %copy-done.4, ...), custom_call_target="tpu_custom_call" | custom-call | tf_op jit(solution)/shard_map/unpack_rims/pallas_call | solution.py:91
  79.7 7.6 %all-to-all-start.1 = ((bf16[16,136,256]{2,1,0:T(8,128)(2,1)}), bf16[16,136,256]{2,1,0:T(8,128)(2,1)S(1)}, u32[]{:S(2)}, u32[]{:S(2)}) async-start(bf16[16,136,256]{2,1,0:T(8,128)(2,1)} %unpack_rims.1), calls=%async_computation.1 | async-start | bytes 2228224 | tf_op jit(solution)/shard_map/all_to_all | solution.py:295
  87.3 0.6 dynamic_slice.6.extent_ref
  87.9 6.5 %inner_cells.1 = (f32[49,8,256]{2,1,0:T(8,128)}, f32[16,136,256]{2,1,0:T(8,128)}) custom-call(f32[1,256]{1,0:T(1,128)} %bitcast.8, bf16[16,4,128,256]{3,2,1,0:T(8,128)(2,1)} %all-to-all-done.main_ref), custom_call_target="tpu_custom_call" | custom-call | tf_op jit(solution)/shard_map/inner_cells/pallas_call | solution.py:180
  94.4 11.7 %all-to-all-done.1.rim_ref = bf16[16,136,256]{2,1,0:T(8,128)(2,1)S(1)} async-done(((bf16[16,136,256]{2,1,0:T(8,128)(2,1)}), bf16[16,136,256]{2,1,0:T(8,128)(2,1)S(1)}, u32[]{:S(2)}, u32[]{:S(2)}) %all-to-all-start.1) | async-done | bytes 1114144 | tf_op jit(solution)/shard_map/all_to_all | solution.py:295
  106.2 1.0 copy-done
  107.2 3.6 %rim_cells.1 = f32[49,8,256]{2,1,0:T(8,128)} custom-call(s32[1]{0:T(128)} %dynamic_slice.6.extent_ref, f32[49,8,256]{2,1,0:T(8,128)} %get-tuple-element.23.in_ref, f32[16,136,256]{2,1,0:T(8,128)} %get-tuple-element.24.side_ref, bf16[16,136,256]{2,1,0:T(8,128)(2,1)} %copy-done), custom_call_target="tpu_custom_call" | custom-call | tf_op jit(solution)/shard_map/rim_cells/pallas_call | solution.py:237
  (47 shorter events, 0.1 us)
Async XLA Ops:
  4.6 7.2 %copy-start.16 = (s32[256,2]{0,1:T(2,128)S(1)}, s32[256,2]{0,1:T(2,128)}, u32[]{:S(2)}) copy-start(s32[256,2]{0,1:T(2,128)} %param.9) | copy-start | bytes 6148
  4.6 7.5 %copy-start.17 = (s32[256,2]{0,1:T(2,128)S(1)}, s32[256,2]{0,1:T(2,128)}, u32[]{:S(2)}) copy-start(s32[256,2]{0,1:T(2,128)} %param.10) | copy-start | bytes 6148
  4.6 75.1 %all-to-all-start = ((bf16[16,4,128,256]{3,2,1,0:T(8,128)(2,1)}), bf16[16,4,128,256]{3,2,1,0:T(8,128)(2,1)}, u32[]{:S(2)}, u32[]{:S(2)}) async-start(bf16[16,4,128,256]{3,2,1,0:T(8,128)(2,1)} %pad_maximum_fusion), calls=%async_computation | async-start | bytes 8388608 | tf_op jit(solution)/shard_map/all_to_all | solution.py:284
  17.8 8.5 %collective-permute-start = (bf16[208,256]{1,0:T(8,128)(2,1)}, bf16[208,256]{1,0:T(8,128)(2,1)S(1)}, u32[]{:S(2)}, u32[]{:S(2)}) collective-permute-start(bf16[208,256]{1,0:T(8,128)(2,1)} %get-tuple-element.26), channel_id=1, source_target_pairs={{0,16},{16,0},{32,48},{48,32},{64,80},{80,64},{96,112},{112,96},{1... | collective-permute-start | bytes 319496 | tf_op jit(solution)/shard_map/ppermute | solution.py:293
  17.8 8.6 %collective-permute-start.1 = (bf16[208,256]{1,0:T(8,128)(2,1)}, bf16[208,256]{1,0:T(8,128)(2,1)S(1)}, u32[]{:S(2)}, u32[]{:S(2)}) collective-permute-start(bf16[208,256]{1,0:T(8,128)(2,1)} %get-tuple-element.27), channel_id=1, source_target_pairs={{0,32},{16,48},{32,64},{48,80},{64,96},{80,112},{96,128},{112,144}... | collective-permute-start | bytes 319496 | tf_op jit(solution)/shard_map/ppermute | solution.py:293
  19.8 11.3 %collective-permute-start.2 = (bf16[208,256]{1,0:T(8,128)(2,1)}, bf16[208,256]{1,0:T(8,128)(2,1)S(1)}, u32[]{:S(2)}, u32[]{:S(2)}) collective-permute-start(bf16[208,256]{1,0:T(8,128)(2,1)} %get-tuple-element.28), channel_id=1, source_target_pairs={{0,48},{16,32},{32,80},{48,64},{64,112},{80,96},{96,144},{112,128}... | collective-permute-start | bytes 319496 | tf_op jit(solution)/shard_map/ppermute | solution.py:293
  21.4 14.3 %collective-permute-start.3 = (bf16[208,256]{1,0:T(8,128)(2,1)}, bf16[208,256]{1,0:T(8,128)(2,1)S(1)}, u32[]{:S(2)}, u32[]{:S(2)}) collective-permute-start(bf16[208,256]{1,0:T(8,128)(2,1)} %get-tuple-element.29), channel_id=1, source_target_pairs={{0,64},{16,80},{32,96},{48,112},{64,128},{80,144},{96,160},{112,17... | collective-permute-start | bytes 319496 | tf_op jit(solution)/shard_map/ppermute | solution.py:293
  25.0 13.7 %collective-permute-start.4 = (bf16[208,256]{1,0:T(8,128)(2,1)}, bf16[208,256]{1,0:T(8,128)(2,1)S(1)}, u32[]{:S(2)}, u32[]{:S(2)}) collective-permute-start(bf16[208,256]{1,0:T(8,128)(2,1)} %get-tuple-element.30), channel_id=1, source_target_pairs={{0,80},{16,64},{32,112},{48,96},{64,144},{80,128},{96,176},{112,16... | collective-permute-start | bytes 319496 | tf_op jit(solution)/shard_map/ppermute | solution.py:293
  26.2 49.2 %copy-start.1 = (bf16[208,256]{1,0:T(8,128)(2,1)}, bf16[208,256]{1,0:T(8,128)(2,1)S(1)}, u32[]{:S(2)}) copy-start(bf16[208,256]{1,0:T(8,128)(2,1)S(1)} %collective-permute-done.refs_1_) | copy-start | bytes 319492
  26.2 23.9 %collective-permute-start.5 = (bf16[208,256]{1,0:T(8,128)(2,1)}, bf16[208,256]{1,0:T(8,128)(2,1)S(1)}, u32[]{:S(2)}, u32[]{:S(2)}) collective-permute-start(bf16[208,256]{1,0:T(8,128)(2,1)} %get-tuple-element.31), channel_id=1, source_target_pairs={{0,96},{16,112},{32,128},{48,144},{64,160},{80,176},{96,192},{112,... | collective-permute-start | bytes 319496 | tf_op jit(solution)/shard_map/ppermute | solution.py:293
  26.4 49.0 %copy-start.2 = (bf16[208,256]{1,0:T(8,128)(2,1)}, bf16[208,256]{1,0:T(8,128)(2,1)S(1)}, u32[]{:S(2)}) copy-start(bf16[208,256]{1,0:T(8,128)(2,1)S(1)} %collective-permute-done.1.refs_2_) | copy-start | bytes 319492
  26.4 26.4 %collective-permute-start.6 = (bf16[208,256]{1,0:T(8,128)(2,1)}, bf16[208,256]{1,0:T(8,128)(2,1)S(1)}, u32[]{:S(2)}, u32[]{:S(2)}) collective-permute-start(bf16[208,256]{1,0:T(8,128)(2,1)} %get-tuple-element.32), channel_id=1, source_target_pairs={{0,112},{16,96},{32,144},{48,128},{64,176},{80,160},{96,208},{112,... | collective-permute-start | bytes 319496 | tf_op jit(solution)/shard_map/ppermute | solution.py:293
  31.1 44.3 %copy-start.3 = (bf16[208,256]{1,0:T(8,128)(2,1)}, bf16[208,256]{1,0:T(8,128)(2,1)S(1)}, u32[]{:S(2)}) copy-start(bf16[208,256]{1,0:T(8,128)(2,1)S(1)} %collective-permute-done.2.refs_3_) | copy-start | bytes 319492
  31.1 21.7 %collective-permute-start.7 = (bf16[208,256]{1,0:T(8,128)(2,1)}, bf16[208,256]{1,0:T(8,128)(2,1)S(1)}, u32[]{:S(2)}, u32[]{:S(2)}) collective-permute-start(bf16[208,256]{1,0:T(8,128)(2,1)} %get-tuple-element.33), channel_id=1, source_target_pairs={{0,128},{16,144},{32,160},{48,176},{64,192},{80,208},{96,224},{112... | collective-permute-start | bytes 319496 | tf_op jit(solution)/shard_map/ppermute | solution.py:293
  35.8 39.6 %copy-start.4 = (bf16[208,256]{1,0:T(8,128)(2,1)}, bf16[208,256]{1,0:T(8,128)(2,1)S(1)}, u32[]{:S(2)}) copy-start(bf16[208,256]{1,0:T(8,128)(2,1)S(1)} %collective-permute-done.3.refs_4_) | copy-start | bytes 319492
  35.8 24.7 %collective-permute-start.8 = (bf16[208,256]{1,0:T(8,128)(2,1)}, bf16[208,256]{1,0:T(8,128)(2,1)S(1)}, u32[]{:S(2)}, u32[]{:S(2)}) collective-permute-start(bf16[208,256]{1,0:T(8,128)(2,1)} %get-tuple-element.34), channel_id=1, source_target_pairs={{0,144},{16,128},{32,176},{48,160},{64,208},{80,192},{96,240},{112... | collective-permute-start | bytes 319496 | tf_op jit(solution)/shard_map/ppermute | solution.py:293
  38.7 36.7 %copy-start.5 = (bf16[208,256]{1,0:T(8,128)(2,1)}, bf16[208,256]{1,0:T(8,128)(2,1)S(1)}, u32[]{:S(2)}) copy-start(bf16[208,256]{1,0:T(8,128)(2,1)S(1)} %collective-permute-done.4.refs_5_) | copy-start | bytes 319492
  38.7 27.3 %collective-permute-start.9 = (bf16[208,256]{1,0:T(8,128)(2,1)}, bf16[208,256]{1,0:T(8,128)(2,1)S(1)}, u32[]{:S(2)}, u32[]{:S(2)}) collective-permute-start(bf16[208,256]{1,0:T(8,128)(2,1)} %get-tuple-element.35), channel_id=1, source_target_pairs={{0,160},{16,176},{32,192},{48,208},{64,224},{80,240},{96,0},{112,1... | collective-permute-start | bytes 319496 | tf_op jit(solution)/shard_map/ppermute | solution.py:293
  50.2 25.2 %copy-start.6 = (bf16[208,256]{1,0:T(8,128)(2,1)}, bf16[208,256]{1,0:T(8,128)(2,1)S(1)}, u32[]{:S(2)}) copy-start(bf16[208,256]{1,0:T(8,128)(2,1)S(1)} %collective-permute-done.5.refs_6_) | copy-start | bytes 319492
  50.2 16.5 %collective-permute-start.10 = (bf16[208,256]{1,0:T(8,128)(2,1)}, bf16[208,256]{1,0:T(8,128)(2,1)S(1)}, u32[]{:S(2)}, u32[]{:S(2)}) collective-permute-start(bf16[208,256]{1,0:T(8,128)(2,1)} %get-tuple-element.36), channel_id=1, source_target_pairs={{0,176},{16,160},{32,208},{48,192},{64,240},{80,224},{96,16},{112,... | collective-permute-start | bytes 319496 | tf_op jit(solution)/shard_map/ppermute | solution.py:293
  52.8 22.7 %copy-start.7 = (bf16[208,256]{1,0:T(8,128)(2,1)}, bf16[208,256]{1,0:T(8,128)(2,1)S(1)}, u32[]{:S(2)}) copy-start(bf16[208,256]{1,0:T(8,128)(2,1)S(1)} %collective-permute-done.6.refs_7_) | copy-start | bytes 319492
  52.8 14.4 %collective-permute-start.11 = (bf16[208,256]{1,0:T(8,128)(2,1)}, bf16[208,256]{1,0:T(8,128)(2,1)S(1)}, u32[]{:S(2)}, u32[]{:S(2)}) collective-permute-start(bf16[208,256]{1,0:T(8,128)(2,1)} %get-tuple-element.37), channel_id=1, source_target_pairs={{0,192},{16,208},{32,224},{48,240},{64,0},{80,16},{96,32},{112,48}... | collective-permute-start | bytes 319496 | tf_op jit(solution)/shard_map/ppermute | solution.py:293
  52.8 22.7 %copy-start.8 = (bf16[208,256]{1,0:T(8,128)(2,1)}, bf16[208,256]{1,0:T(8,128)(2,1)S(1)}, u32[]{:S(2)}) copy-start(bf16[208,256]{1,0:T(8,128)(2,1)S(1)} %collective-permute-done.7.refs_8_) | copy-start | bytes 319492
  52.8 15.6 %collective-permute-start.12 = (bf16[208,256]{1,0:T(8,128)(2,1)}, bf16[208,256]{1,0:T(8,128)(2,1)S(1)}, u32[]{:S(2)}, u32[]{:S(2)}) collective-permute-start(bf16[208,256]{1,0:T(8,128)(2,1)} %get-tuple-element.38), channel_id=1, source_target_pairs={{0,208},{16,192},{32,240},{48,224},{64,16},{80,0},{96,48},{112,32}... | collective-permute-start | bytes 319496 | tf_op jit(solution)/shard_map/ppermute | solution.py:293
  60.5 14.9 %copy-start.9 = (bf16[208,256]{1,0:T(8,128)(2,1)}, bf16[208,256]{1,0:T(8,128)(2,1)S(1)}, u32[]{:S(2)}) copy-start(bf16[208,256]{1,0:T(8,128)(2,1)S(1)} %collective-permute-done.8.refs_9_) | copy-start | bytes 319492
  60.5 13.3 %collective-permute-start.13 = (bf16[208,256]{1,0:T(8,128)(2,1)}, bf16[208,256]{1,0:T(8,128)(2,1)S(1)}, u32[]{:S(2)}, u32[]{:S(2)}) collective-permute-start(bf16[208,256]{1,0:T(8,128)(2,1)} %get-tuple-element.39), channel_id=1, source_target_pairs={{0,224},{16,240},{32,0},{48,16},{64,32},{80,48},{96,64},{112,80},{... | collective-permute-start | bytes 319496 | tf_op jit(solution)/shard_map/ppermute | solution.py:293
  66.0 9.4 %copy-start.10 = (bf16[208,256]{1,0:T(8,128)(2,1)}, bf16[208,256]{1,0:T(8,128)(2,1)S(1)}, u32[]{:S(2)}) copy-start(bf16[208,256]{1,0:T(8,128)(2,1)S(1)} %collective-permute-done.9.refs_10_) | copy-start | bytes 319492
  66.0 9.3 %collective-permute-start.14 = (bf16[208,256]{1,0:T(8,128)(2,1)}, bf16[208,256]{1,0:T(8,128)(2,1)S(1)}, u32[]{:S(2)}, u32[]{:S(2)}) collective-permute-start(bf16[208,256]{1,0:T(8,128)(2,1)} %get-tuple-element.40), channel_id=1, source_target_pairs={{0,240},{16,224},{32,16},{48,0},{64,48},{80,32},{96,80},{112,64},{... | collective-permute-start | bytes 319496 | tf_op jit(solution)/shard_map/ppermute | solution.py:293
  66.7 8.8 %copy-start.11 = (bf16[208,256]{1,0:T(8,128)(2,1)}, bf16[208,256]{1,0:T(8,128)(2,1)S(1)}, u32[]{:S(2)}) copy-start(bf16[208,256]{1,0:T(8,128)(2,1)S(1)} %collective-permute-done.10.refs_11_) | copy-start | bytes 319492
  67.1 8.3 %copy-start.12 = (bf16[208,256]{1,0:T(8,128)(2,1)}, bf16[208,256]{1,0:T(8,128)(2,1)S(1)}, u32[]{:S(2)}) copy-start(bf16[208,256]{1,0:T(8,128)(2,1)S(1)} %collective-permute-done.11.refs_12_) | copy-start | bytes 319492
  68.4 7.1 %copy-start.13 = (bf16[208,256]{1,0:T(8,128)(2,1)}, bf16[208,256]{1,0:T(8,128)(2,1)S(1)}, u32[]{:S(2)}) copy-start(bf16[208,256]{1,0:T(8,128)(2,1)S(1)} %collective-permute-done.12.refs_13_) | copy-start | bytes 319492
  73.8 1.7 %copy-start.14 = (bf16[208,256]{1,0:T(8,128)(2,1)}, bf16[208,256]{1,0:T(8,128)(2,1)S(1)}, u32[]{:S(2)}) copy-start(bf16[208,256]{1,0:T(8,128)(2,1)S(1)} %collective-permute-done.13.refs_14_) | copy-start | bytes 319492
  75.4 0.6 copy-start.15
  76.0 11.3 %copy-start.18 = (s32[16]{0:T(128)S(1)}, s32[16]{0:T(128)}, u32[]{:S(2)}) copy-start(s32[16]{0:T(128)} %param.11) | copy-start | bytes 196
  79.7 26.5 %all-to-all-start.1 = ((bf16[16,136,256]{2,1,0:T(8,128)(2,1)}), bf16[16,136,256]{2,1,0:T(8,128)(2,1)S(1)}, u32[]{:S(2)}, u32[]{:S(2)}) async-start(bf16[16,136,256]{2,1,0:T(8,128)(2,1)} %unpack_rims.1), calls=%async_computation.1 | async-start | bytes 2228224 | tf_op jit(solution)/shard_map/all_to_all | solution.py:295
  106.2 1.0 copy-start
